TPU v7x, 32 devices: a whole 2x2x4 slice. The times are simulated.
32 devices in a mesh: slab: 8 (over y, x, core), grp: 4 (over z).
Axes of the slice: x: 2, y: 2, z: 4, core: 2. Of those that a mesh axis runs over, the one named last changes fastest.
Arguments:
- near_field: bfloat16 [2, 4096, 2048], P(None, 'slab', 'grp'), may hold values from -6 to 6
- lens_phase: float32 [2, 4096, 2048], P(None, 'slab', 'grp'), may hold values from -3.140625 to 3.140625
Outputs:
- far_field: float32 [2, 512, 2048], P(None, ('slab', 'grp'))
All inputs are finite; a program needn't handle non-finite values.
Results may differ from a plain program's by a relative error of at most 0.0083.
Values may be sent and summed in bfloat16 or wider, within the bound.
A program may use at most 128 MiB of HBM per device.

v0:
```python
import math

import jax
import jax.numpy as jnp
from jax import lax
from jax.sharding import PartitionSpec as P

NV = 2048
AV = 512
AL = 2048
STEPS = 2
LAT_DEV = 512


def phase_table(row_index, col_index, modulus):
    turns = jnp.mod(row_index[:, None] * col_index[None, :], modulus)
    angle = turns.astype(jnp.float32) * (2.0 * math.pi / modulus)
    return (jnp.cos(angle).astype(jnp.bfloat16), jnp.sin(angle).astype(jnp.bfloat16))


def propagator():
    wave_index = jnp.arange(NV, dtype=jnp.int32)
    offset = wave_index[None, :] - wave_index[:, None]
    turns = jnp.mod(offset * offset, 2 * NV)
    angle = turns.astype(jnp.float32) * (math.pi / NV) - math.pi / 4.0
    gain = 1.0 / math.sqrt(NV)
    return (
        (jnp.cos(angle) * gain).astype(jnp.bfloat16),
        (jnp.sin(angle) * gain).astype(jnp.bfloat16),
    )


def matmul(left, right):
    return jnp.dot(left, right, preferred_element_type=jnp.float32)


def to_rows(field):
    return lax.all_to_all(field, "grp", split_axis=1, concat_axis=2, tiled=True)


def apply_lens(propagated, phase):
    lens_cos = jnp.cos(phase)
    lens_sin = jnp.sin(phase)
    prop_real = propagated[0].astype(jnp.float32)
    prop_imag = propagated[1].astype(jnp.float32)
    new_real = (prop_real * lens_cos - prop_imag * lens_sin).astype(jnp.bfloat16)
    new_imag = (prop_real * lens_sin + prop_imag * lens_cos).astype(jnp.bfloat16)
    return jnp.stack([new_real, new_imag])


def lateral_sum(col_real, col_imag, row_global, total_rows):
    lat_cos, lat_sin = phase_table(
        row_global - total_rows // 2, jnp.arange(AL, dtype=jnp.int32) - AL // 2, 2 * total_rows
    )
    out_real = jnp.einsum("na,nj->aj", col_real, lat_cos, preferred_element_type=jnp.float32)
    out_real = out_real + jnp.einsum(
        "na,nj->aj", col_imag, lat_sin, preferred_element_type=jnp.float32
    )
    out_imag = jnp.einsum("na,nj->aj", col_imag, lat_cos, preferred_element_type=jnp.float32)
    out_imag = out_imag - jnp.einsum(
        "na,nj->aj", col_real, lat_sin, preferred_element_type=jnp.float32
    )
    return (out_real, out_imag)


def on_device(near_field, lens_phase):
    slab_count = lax.axis_size("slab")
    group_count = lax.axis_size("grp")
    total_rows = LAT_DEV * slab_count
    row_count = LAT_DEV // group_count
    scale = 1.0 / math.sqrt(total_rows * NV)
    wave_index = jnp.arange(NV, dtype=jnp.int32)
    prop_cos, prop_sin = propagator()
    field = near_field
    for section in range(STEPS):
        propagate_field = to_rows(field)
        prop_real = (
            matmul(propagate_field[0], prop_cos) - matmul(propagate_field[1], prop_sin)
        ).astype(jnp.bfloat16)
        prop_imag = (
            matmul(propagate_field[0], prop_sin) + matmul(propagate_field[1], prop_cos)
        ).astype(jnp.bfloat16)
        propagated = jnp.stack([prop_real, prop_imag])
        back = lax.all_to_all(propagated, "grp", split_axis=2, concat_axis=1, tiled=True)
        field = apply_lens(back, lens_phase[section])
    rows = to_rows(field)
    vert_cos, vert_sin = phase_table(
        wave_index - NV // 2, jnp.arange(AV, dtype=jnp.int32) - AV // 2, 2 * NV
    )
    col_real = (matmul(rows[0], vert_cos) + matmul(rows[1], vert_sin)).astype(jnp.bfloat16)
    col_imag = (matmul(rows[1], vert_cos) - matmul(rows[0], vert_sin)).astype(jnp.bfloat16)
    slab_index = lax.axis_index("slab")
    group_index = lax.axis_index("grp")
    row_global = (
        slab_index * LAT_DEV + group_index * row_count + jnp.arange(row_count, dtype=jnp.int32)
    )
    out_real, out_imag = lateral_sum(col_real, col_imag, row_global, total_rows)
    partial_sum = jnp.stack([out_real, out_imag]) * scale
    return lax.psum_scatter(partial_sum, ("slab", "grp"), scatter_dimension=1, tiled=True)


def solution(mesh):
    return jax.shard_map(
        on_device,
        mesh=mesh,
        in_specs=(P(None, "slab", "grp"), P(None, "slab", "grp")),
        out_specs=P(None, ("slab", "grp"), None),
        check_vma=False,
    )
```

profile of v0, /device:TPU:0, one launch (start us, length us, event | category | flops | bytes accessed | tf_op | source)
XLA Modules:
  0.0 980.6 jit_solution(12029729377742225466)
XLA Ops:
  6.5 2.3 copy.53
  8.8 31.9 %all_to_all.75 = bf16[2,512,512]{2,0,1:T(2,128)(2,1)S(1)} all-to-all(bf16[2,512,512]{2,0,1:T(2,128)(2,1)S(1)} %copy.53), channel_id=1, replica_groups=mesh['slab'=8,'grp'=4] {'grp'}, dimensions={1} | all-to-all | bytes 2097152 | tf_op jit(solution)/shard_map/all_to_all | solution.py:38
  40.7 0.2 copy.54
  40.9 0.1 fusion.132
  41.0 0.3 copy.55
  41.2 0.3 copy.56
  41.5 66.0 %fusion.6 = f32[2048,128]{1,0:T(8,128)S(1)} fusion(bf16[128,2048]{0,1:T(8,128)(2,1)S(1)} %bitcast.88), kind=kOutput, calls=%fused_computation.12 | convolution fusion | flops 1149239296 | bytes 1572864 | tf_op jit(solution)/shard_map/dot_general | solution.py:34
  107.5 66.0 %fusion.7 = f32[2048,128]{1,0:T(8,128)S(1)} fusion(bf16[128,2048]{0,1:T(8,128)(2,1)S(1)} %bitcast.86), kind=kOutput, calls=%fused_computation.13 | convolution fusion | flops 1149239296 | bytes 1572864 | tf_op jit(solution)/shard_map/dot_general | solution.py:34
  173.6 66.8 %fusion.24 = bf16[1,128,2048]{1,2,0:T(8,128)(2,1)S(1)} fusion(f32[2048,128]{1,0:T(8,128)S(1)} %fusion.6, bf16[128,2048]{0,1:T(8,128)(2,1)S(1)} %bitcast.87), kind=kOutput, calls=%fused_computation.39 | convolution fusion | flops 1149763584 | bytes 2097152 | tf_op jit(solution)/shard_map/dot_general | solution.py:34
  240.4 66.6 %fusion.23 = bf16[1,128,2048]{1,2,0:T(8,128)(2,1)S(1)} fusion(f32[2048,128]{1,0:T(8,128)S(1)} %fusion.7, bf16[128,2048]{0,1:T(8,128)(2,1)S(1)} %bitcast.89), kind=kOutput, calls=%fused_computation.38 | convolution fusion | flops 1149763584 | bytes 2097152 | tf_op jit(solution)/shard_map/dot_general | solution.py:34
  307.0 0.1 pad_maximum_fusion
  307.1 8.9 copy.57
  316.0 27.8 %all_to_all.76 = bf16[2,128,2048]{1,0,2:T(2,128)(2,1)S(1)} all-to-all(bf16[2,128,2048]{1,0,2:T(2,128)(2,1)S(1)} %copy.57), channel_id=1, replica_groups=mesh['slab'=8,'grp'=4] {'grp'}, dimensions={2} | all-to-all | bytes 2097152 | tf_op jit(solution)/shard_map/all_to_all | solution.py:84
  343.9 0.8 copy.59
  344.7 0.1 fusion.131
  344.7 5.0 fusion.36
  349.8 0.1 pad_maximum_fusion.1
  349.9 1.1 copy.60
  351.0 28.1 %all_to_all.77 = bf16[2,512,512]{2,0,1:T(2,128)(2,1)S(1)} all-to-all(bf16[2,512,512]{2,0,1:T(2,128)(2,1)S(1)} %copy.60), channel_id=1, replica_groups=mesh['slab'=8,'grp'=4] {'grp'}, dimensions={1} | all-to-all | bytes 2097152 | tf_op jit(solution)/shard_map/all_to_all | solution.py:38
  379.0 0.2 copy.61
  379.2 0.1 fusion.130
  379.3 0.3 copy.62
  379.6 0.3 copy.63
  379.8 64.0 %fusion.4 = f32[128,2048]{1,0:T(8,128)S(1)} fusion(bf16[128,2048]{0,1:T(8,128)(2,1)S(1)} %bitcast.92), kind=kOutput, calls=%fused_computation.10 | convolution fusion | flops 1149239296 | bytes 1572864 | tf_op jit(solution)/shard_map/dot_general | solution.py:34
  443.9 64.5 %fusion.5 = f32[128,2048]{1,0:T(8,128)S(1)} fusion(bf16[128,2048]{0,1:T(8,128)(2,1)S(1)} %bitcast.90), kind=kOutput, calls=%fused_computation.11 | convolution fusion | flops 1149239296 | bytes 1572864 | tf_op jit(solution)/shard_map/dot_general | solution.py:34
  508.4 64.7 %fusion.26 = bf16[1,128,2048]{2,1,0:T(8,128)(2,1)S(1)} fusion(f32[128,2048]{1,0:T(8,128)S(1)} %fusion.4, bf16[128,2048]{0,1:T(8,128)(2,1)S(1)} %bitcast.91), kind=kOutput, calls=%fused_computation.41 | convolution fusion | flops 1149763584 | bytes 2097152 | tf_op jit(solution)/shard_map/dot_general | solution.py:34
  573.1 64.8 %fusion.25 = bf16[1,128,2048]{2,1,0:T(8,128)(2,1)S(1)} fusion(f32[128,2048]{1,0:T(8,128)S(1)} %fusion.5, bf16[128,2048]{0,1:T(8,128)(2,1)S(1)} %bitcast.93), kind=kOutput, calls=%fused_computation.40 | convolution fusion | flops 1149763584 | bytes 2097152 | tf_op jit(solution)/shard_map/dot_general | solution.py:34
  637.8 0.1 pad_maximum_fusion.2
  638.0 0.8 copy.64
  638.8 27.8 %all_to_all.78 = bf16[2,128,2048]{1,0,2:T(2,128)(2,1)S(1)} all-to-all(bf16[2,128,2048]{1,0,2:T(2,128)(2,1)S(1)} %copy.64), channel_id=1, replica_groups=mesh['slab'=8,'grp'=4] {'grp'}, dimensions={2} | all-to-all | bytes 2097152 | tf_op jit(solution)/shard_map/all_to_all | solution.py:84
  666.6 0.8 copy.66
  667.4 0.1 fusion.129
  667.4 5.0 fusion.40
  672.5 0.1 pad_maximum_fusion.3
  672.6 2.0 copy.67
  674.6 3.5 all-to-all-start.4
  678.1 0.4 reduce-scatter.2.cloned.1.call-start
  678.6 24.2 %all-to-all-done.4 = bf16[2,512,512]{2,0,1:T(2,128)(2,1)S(1)} async-done(((bf16[2,512,512]{2,0,1:T(2,128)(2,1)}), bf16[2,512,512]{2,0,1:T(2,128)(2,1)S(1)}, u32[]{:S(2)}, u32[]{:S(2)}) %all-to-all-start.4) | async-done | bytes 1048608 | tf_op jit(solution)/shard_map/all_to_all | solution.py:38
  702.9 0.2 copy.68
  703.0 0.1 fusion.128
  703.1 0.3 copy.69
  703.4 0.3 copy.70
  703.7 15.6 %fusion.28 = f32[128,512]{1,0:T(8,128)S(1)} fusion(bf16[128,2048]{0,1:T(8,128)(2,1)S(1)} %bitcast.84, s32[512]{0:T(512)S(1)} %iota_add_fusion.1, s32[2048]{0:T(1024)S(1)} %iota_add_fusion), kind=kOutput, calls=%fused_computation.43 | convolution fusion | flops 284164096 | bytes 796672 | tf_op jit(solution)/shard_map/dot_general | solution.py:34
  719.2 15.6 %fusion.27 = f32[128,512]{1,0:T(8,128)S(1)} fusion(bf16[128,2048]{0,1:T(8,128)(2,1)S(1)} %bitcast.94, s32[512]{0:T(512)S(1)} %iota_add_fusion.1, s32[2048]{0:T(1024)S(1)} %iota_add_fusion), kind=kOutput, calls=%fused_computation.42 | convolution fusion | flops 284164096 | bytes 796672 | tf_op jit(solution)/shard_map/dot_general | solution.py:34
  734.8 16.1 %fusion.34 = bf16[128,512]{1,0:T(8,128)(2,1)S(1)} fusion(f32[128,512]{1,0:T(8,128)S(1)} %fusion.28, bf16[128,2048]{0,1:T(8,128)(2,1)S(1)} %bitcast.95, s32[512]{0:T(512)S(1)} %iota_add_fusion.1, s32[2048]{0:T(1024)S(1)} %iota_add_fusion), kind=kOutput, calls=%fused_computation.62 | convolution fusion | flops 284295168 | bytes 927744 | tf_op jit(solution)/shard_map/dot_general | solution.py:34
  750.9 15.7 %fusion.33 = bf16[128,512]{1,0:T(8,128)(2,1)S(1)} fusion(f32[128,512]{1,0:T(8,128)S(1)} %fusion.27, bf16[128,2048]{0,1:T(8,128)(2,1)S(1)} %bitcast.85, s32[512]{0:T(512)S(1)} %iota_add_fusion.1, s32[2048]{0:T(1024)S(1)} %iota_add_fusion), kind=kOutput, calls=%fused_computation.61 | convolution fusion | flops 284295168 | bytes 927744 | tf_op jit(solution)/shard_map/dot_general | solution.py:34
  766.7 4.2 fusion.46
  770.9 4.4 fusion.47
  775.3 4.4 subtract_bitcast_fusion
  779.7 4.4 add_bitcast_fusion
  784.1 4.2 maximum_multiply_fusion
  788.3 0.0 reduce-scatter.2.cloned.1.call-update
  788.3 185.0 %reduce-scatter.2.cloned.1.call-done = f32[2,16,2048]{2,1,0:T(8,128)} async-done(((f32[2,512,2048]{2,1,0:T(8,128)}), f32[2,16,2048]{2,1,0:T(8,128)}) %reduce-scatter.2.cloned.1.call-update) | async-done | bytes 262160 | tf_op jit(solution)/shard_map/reduce_scatter | solution.py:99
  (3 shorter events, 0.0 us)
Async XLA Ops:
  674.6 28.2 %all-to-all-start.4 = ((bf16[2,512,512]{2,0,1:T(2,128)(2,1)}), bf16[2,512,512]{2,0,1:T(2,128)(2,1)S(1)}, u32[]{:S(2)}, u32[]{:S(2)}) async-start(bf16[2,512,512]{2,0,1:T(2,128)(2,1)} %copy.67), calls=%async_computation.4 | async-start | bytes 2097152 | tf_op jit(solution)/shard_map/all_to_all | solution.py:38
  678.1 295.2 %reduce-scatter.2.cloned.1.call-start = ((), (), s32[]{:S(2)}) async-start(), calls=%async_computation.6 | async-start | bytes 8650752 | tf_op jit(solution)/shard_map/reduce_scatter | solution.py:99
Sparse Core Ops, SparseCore 0:
  788.5 184.8 reduce-scatter.1
where the time goes:
time: 989 us; the launch traced here: 981 us
  matrix products  604 us (61%)
  waiting for transfers between devices  209 us (21%)
  blocking collectives  116 us (12%)
  local copies, waits for them, and re-layouts  19.2 us (2%)
  other arithmetic  14.6 us (1%)
  between operations  14.2 us (1%)
    dot_general x12, matrix products, matmul(): return jnp.dot(left, right, preferred_element_type=jnp.float32)  586 us
    reduce_scatter x1, waiting for transfers between devices, on_device(): lax.psum_scatter(partial_sum, ('slab', 'grp'), scatter_dimension=1, tiled...  185 us
    all_to_all x2, blocking collectives, to_rows(): return lax.all_to_all(field, 'grp', split_axis=1, concat_axis=2, tiled=True)  60 us
    all_to_all x2, blocking collectives, on_device(): lax.all_to_all(propagated, 'grp', split_axis=2, concat_axis=1, tiled=True)  55.6 us
    all_to_all x1, waiting for transfers between devices, to_rows(): return lax.all_to_all(field, 'grp', split_axis=1, concat_axis=2, tiled=True)  24.2 us
  transfers between devices with their start and end apart: 2, of which 2 were waited for; matrix products, arithmetic and copies ran while one was open for 0% of the time, Pallas kernels for 0%

commit v1 on v0

v1 whole, which is shorter than its diff:
```python
import math

import jax
import jax.numpy as jnp
from jax import lax
from jax.sharding import PartitionSpec as P

AV = 512
AL = 2048
PHASE_CODE = 40.0


def sincos(angle):
    half = 0.5 * angle
    sq = half * half
    sin = -1.0 / 39916800.0
    for term in (1.0 / 362880.0, -1.0 / 5040.0, 1.0 / 120.0, -1.0 / 6.0, 1.0):
        sin = sin * sq + term
    sin = sin * half
    cos = 1.0 / 479001600.0
    for term in (-1.0 / 3628800.0, 1.0 / 40320.0, -1.0 / 720.0, 1.0 / 24.0, -0.5, 1.0):
        cos = cos * sq + term
    return 1.0 - 2.0 * sin * sin, 2.0 * sin * cos


def unit_angle(turns, modulus):
    assert modulus & (modulus - 1) == 0
    centred = ((turns + modulus // 2) & (modulus - 1)) - modulus // 2
    return sincos(centred.astype(jnp.float32) * (2.0 * math.pi / modulus))


def count(size):
    return lax.optimization_barrier(jnp.arange(size, dtype=jnp.int32))


def phase_table(row_index, col_index, modulus):
    cos, sin = unit_angle(row_index[:, None] * col_index[None, :], modulus)
    return cos.astype(jnp.bfloat16), sin.astype(jnp.bfloat16)


def propagator(points):
    band = math.gcd(points, 128)
    offset = count(points)[None, :] - count(band)[:, None]
    cos, sin = unit_angle(offset * offset - points // 4, 2 * points)
    gain = 1.0 / math.sqrt(points)

    def rolled(part):
        part = lax.optimization_barrier((part * gain).astype(jnp.bfloat16))
        twice = jnp.concatenate([part, part], axis=1)
        return jnp.concatenate(
            [
                lax.slice_in_dim(twice, points - start, 2 * points - start, axis=1)
                for start in range(0, points, band)
            ]
        )

    return rolled(cos), rolled(sin)


def matmul(left, right):
    return jnp.dot(left, right, preferred_element_type=jnp.float32)


def complex_product(both, table_cos, table_sin):
    rows = both.shape[0] // 2
    with_cos = matmul(both, table_cos)
    with_sin = matmul(both, table_sin)
    return with_cos[:rows] - with_sin[rows:], with_sin[:rows] + with_cos[rows:]


def on_device(near_field, lens_phase):
    slab_count = lax.axis_size("slab")
    group_count = lax.axis_size("grp")
    devices = slab_count * group_count
    steps, lat_dev, width = lens_phase.shape
    points = width * group_count
    total_rows = lat_dev * slab_count
    rows = lat_dev // group_count
    angles = AV // devices
    coded = [jnp.exp2(lens_phase[k] * PHASE_CODE).astype(jnp.bfloat16) for k in range(steps)]
    field = lax.all_to_all(near_field, "grp", split_axis=1, concat_axis=2, tiled=True)
    coded = [
        lax.all_to_all(part, "grp", split_axis=0, concat_axis=1, tiled=True) for part in coded
    ]
    prop_cos, prop_sin = propagator(points)
    both = field.reshape(2 * rows, points)
    for section in range(steps):
        real, imag = complex_product(both, prop_cos, prop_sin)
        real = real.astype(jnp.bfloat16).astype(jnp.float32)
        imag = imag.astype(jnp.bfloat16).astype(jnp.float32)
        phase = jnp.log2(coded[section].astype(jnp.float32)) * (1.0 / PHASE_CODE)
        lens_cos, lens_sin = sincos(phase)
        both = jnp.concatenate(
            [
                (real * lens_cos - imag * lens_sin).astype(jnp.bfloat16),
                (real * lens_sin + imag * lens_cos).astype(jnp.bfloat16),
            ]
        )
    vert_cos, vert_sin = phase_table(
        count(points) - points // 2,
        count(AV) - AV // 2,
        2 * points,
    )
    col_real, col_imag = complex_product(both, vert_cos, -vert_sin)
    cols = jnp.stack([col_real, col_imag]).astype(jnp.bfloat16)
    cols = jnp.transpose(cols.reshape(2, rows, devices, angles), (2, 0, 3, 1))
    got = lax.all_to_all(cols, ("slab", "grp"), split_axis=0, concat_axis=0, tiled=True)
    modulus = 2 * total_rows
    period = modulus // rows
    source = count(devices) - devices // 2
    fine = count(period)
    near = count(rows)
    coarse = count(AL // period)
    w_cos, w_sin = phase_table(source, fine, period)
    got_real = got[:, 0]
    got_imag = got[:, 1]
    ein = lambda s, l, r: jnp.einsum(s, l, r, preferred_element_type=jnp.float32)
    mid_real = ein("sam,sf->afm", got_real, w_cos) + ein("sam,sf->afm", got_imag, w_sin)
    mid_imag = ein("sam,sf->afm", got_imag, w_cos) - ein("sam,sf->afm", got_real, w_sin)
    t_cos, t_sin = unit_angle(fine[:, None] * near[None, :], modulus)
    turned_real = (mid_real * t_cos + mid_imag * t_sin).astype(jnp.bfloat16)
    turned_imag = (mid_imag * t_cos - mid_real * t_sin).astype(jnp.bfloat16)
    e_cos, e_sin = phase_table(near, coarse * period - AL // 2, modulus)
    out_real = ein("afm,mc->acf", turned_real, e_cos) + ein("afm,mc->acf", turned_imag, e_sin)
    out_imag = ein("afm,mc->acf", turned_imag, e_cos) - ein("afm,mc->acf", turned_real, e_sin)
    scale = 1.0 / math.sqrt(total_rows * points)
    return (jnp.stack([out_real, out_imag]) * scale).reshape(2, angles, AL)


def solution(mesh):
    return jax.shard_map(
        on_device,
        mesh=mesh,
        in_specs=(P(None, "slab", "grp"), P(None, "slab", "grp")),
        out_specs=P(None, ("slab", "grp"), None),
        check_vma=False,
    )
```

time: 989 us -> 124 us (0.13)
  matrix products: 604 us -> 31.3 us
  waiting for transfers between devices: 209 us -> 43.7 us
  blocking collectives: 116 us -> 0 us
  between operations: 14.2 us -> 0.43 us
  local copies, waits for them, and re-layouts: 19.2 us -> 5.58 us
  starting transfers between devices: 3.96 us -> 17.2 us
  other arithmetic: 14.6 us -> 25.2 us
    dot_general x12 -> x6, matrix products: 586 us -> 28.3 us  [matmul(): return jnp.dot(left, right, preferred_element_type=jnp.float32)]
    reduce_scatter x1 -> x0, waiting for transfers between devices: 185 us -> none  [on_device(): lax.psum_scatter(partial_sum, ('slab', 'grp'), scatter_dimension=1, tiled...]
    all_to_all x4 -> x0, blocking collectives: 116 us -> none  [the longest x2 60 us: to_rows(): return lax.all_to_all(field, 'grp', split_axis=1, concat_axis=2, tiled=True)]
    all_to_all x1 -> x4, waiting for transfers between devices: 24.2 us -> 43.7 us  [the longest x1 20.1 us: on_device(): lax.all_to_all(near_field, 'grp', split_axis=1, concat_axis=2, tiled=True)]
    dot_general x4 -> x8, matrix products: 17.4 us -> 2.97 us  [on_device(): jnp.einsum(s, l, r, preferred_element_type=jnp.float32)]
    unnamed x0 -> x31, other arithmetic: none -> 14.3 us
    all_to_all x1 -> x4, starting transfers between devices: 3.51 us -> 17.2 us  [the longest x2 9.82 us: on_device(): lax.all_to_all(part, 'grp', split_axis=0, concat_axis=1, tiled=True)]
    another operation x4, local copies, waits for them, and re-layouts: 12.8 us -> 0.5 us  [the longest x2 0.26 us: on_device(): return (jnp.stack([out_real, out_imag]) * scale).reshape(2, angles, AL)]
  transfers between devices with their start and end apart: 2 -> 4, of which waited for: 2 -> 4; matrix products, arithmetic and copies ran while one was open for 0% -> 16% of each run, Pallas kernels for 0% -> 0%
where the time goes in v1:
time: 124 us; the launch traced here: 123 us
  waiting for transfers between devices  43.7 us (35%)
  matrix products  31.3 us (25%)
  other arithmetic  25.2 us (20%)
  starting transfers between devices  17.2 us (14%)
  local copies, waits for them, and re-layouts  5.58 us (4%)
    dot_general x6, matrix products, matmul(): return jnp.dot(left, right, preferred_element_type=jnp.float32)  28.3 us
    all_to_all x1, waiting for transfers between devices, on_device(): lax.all_to_all(near_field, 'grp', split_axis=1, concat_axis=2, tiled=True)  20.1 us
    unnamed x31, other arithmetic  14.3 us
    all_to_all x2, waiting for transfers between devices, on_device(): lax.all_to_all(part, 'grp', split_axis=0, concat_axis=1, tiled=True)  13.5 us
    all_to_all x1, waiting for transfers between devices, on_device(): lax.all_to_all(cols, ('slab', 'grp'), split_axis=0, concat_axis=0, tiled=...  10.1 us
    all_to_all x2, starting transfers between devices, on_device(): lax.all_to_all(part, 'grp', split_axis=0, concat_axis=1, tiled=True)  9.82 us
    all_to_all x1, starting transfers between devices, on_device(): lax.all_to_all(cols, ('slab', 'grp'), split_axis=0, concat_axis=0, tiled=...  3.71 us
    all_to_all x1, starting transfers between devices, on_device(): lax.all_to_all(near_field, 'grp', split_axis=1, concat_axis=2, tiled=True)  3.7 us
  transfers between devices with their start and end apart: 4, of which 4 were waited for; matrix products, arithmetic and copies ran while one was open for 16% of the time, Pallas kernels for 0%

profile of v1, /device:TPU:0, one launch (start us, length us, event | category | flops | bytes accessed | tf_op | source)
XLA Modules:
  0.0 123.4 jit_solution(17463661891979874556)
XLA Ops:
  0.0 2.8 %exponential_convert_fusion.1 = (bf16[1,512,512]{2,1,0:T(8,128)(2,1)}, bf16[1,512,512]{2,1,0:T(8,128)(2,1)}) fusion(f32[2,512,512]{2,1,0:T(8,128)} %param.3), kind=kLoop, calls=%fused_computation.138 | loop fusion | flops 1048576 | bytes 3145728 | tf_op jit(solution)/shard_map/convert_element_type | solution.py:80
  2.8 6.3 %all-to-all-start.1 = ((bf16[4,128,512]{2,1,0:T(8,128)(2,1)}), bf16[4,128,512]{2,1,0:T(8,128)(2,1)S(1)}, u32[]{:S(2)}, u32[]{:S(2)}) async-start(bf16[4,128,512]{2,1,0:T(8,128)(2,1)} %bitcast.6), calls=%async_computation.1 | async-start | bytes 1048576 | tf_op jit(solution)/shard_map/all_to_all | solution.py:83
  9.2 1.4 %fusion.27 = (bf16[128,2048]{1,0:T(8,128)(2,1)S(1)}, bf16[128,2048]{1,0:T(8,128)(2,1)S(1)}) fusion(s32[128]{0:T(128)S(1)} %iota.18, s32[2048]{0:T(1024)S(1)} %iota.21), kind=kLoop, calls=%fused_computation.108 | loop fusion | flops 10223616 | bytes 1057280 | tf_op jit(solution)/shard_map/convert_element_type | solution.py:48
  11.3 0.0 copy-start.2
  11.3 0.9 constant_dynamic-update-slice_fusion
  12.2 1.3 %fusion.76 = bf16[2048,2048]{1,0:T(8,128)(2,1)} fusion(bf16[2048,2048]{1,0:T(8,128)(2,1)} %constant_dynamic-update-slice_fusion, bf16[128,2048]{1,0:T(8,128)(2,1)S(1)} %get-tuple-element.20), kind=kLoop, calls=%fused_computation.180 | loop fusion | flops 1048576 | bytes 1048576
  13.6 0.8 fusion.78
  14.4 0.9 fusion.80
  15.3 0.8 fusion.82
  16.1 0.8 fusion.84
  16.9 0.8 fusion.86
  17.8 0.9 fusion.88
  18.6 0.0 copy-done.2
  18.6 0.9 fusion.90
  19.5 4.1 %all-to-all-done.1 = bf16[4,128,512]{2,1,0:T(8,128)(2,1)S(1)} async-done(((bf16[4,128,512]{2,1,0:T(8,128)(2,1)}), bf16[4,128,512]{2,1,0:T(8,128)(2,1)S(1)}, u32[]{:S(2)}, u32[]{:S(2)}) %all-to-all-start.1) | async-done | bytes 524320 | tf_op jit(solution)/shard_map/all_to_all | solution.py:83
  23.6 3.5 %all-to-all-start.2 = ((bf16[4,128,512]{2,1,0:T(8,128)(2,1)}), bf16[4,128,512]{2,1,0:T(8,128)(2,1)S(1)}, u32[]{:S(2)}, u32[]{:S(2)}) async-start(bf16[4,128,512]{2,1,0:T(8,128)(2,1)} %bitcast.8), calls=%async_computation.2 | async-start | bytes 1048576 | tf_op jit(solution)/shard_map/all_to_all | solution.py:83
  27.1 0.0 copy-done.1
  27.1 2.1 %copy.14 = bf16[2,512,512]{2,0,1:T(2,128)(2,1)} copy(bf16[2,512,512]{2,1,0:T(8,128)(2,1)S(1)} %copy-done.1) | data formatting | bytes 2097152 | tf_op args[0]
  29.2 0.8 fusion.92
  30.1 0.9 fusion.94
  30.9 0.9 fusion.96
  31.8 9.4 %all-to-all-done.2 = bf16[4,128,512]{2,1,0:T(8,128)(2,1)S(1)} async-done(((bf16[4,128,512]{2,1,0:T(8,128)(2,1)}), bf16[4,128,512]{2,1,0:T(8,128)(2,1)S(1)}, u32[]{:S(2)}, u32[]{:S(2)}) %all-to-all-start.2) | async-done | bytes 524320 | tf_op jit(solution)/shard_map/all_to_all | solution.py:83
  41.1 3.7 %all-to-all-start = ((bf16[2,512,512]{2,0,1:T(2,128)(2,1)}), bf16[2,512,512]{2,0,1:T(2,128)(2,1)S(1)}, u32[]{:S(2)}, u32[]{:S(2)}) async-start(bf16[2,512,512]{2,0,1:T(2,128)(2,1)} %copy.14), calls=%async_computation | async-start | bytes 2097152 | tf_op jit(solution)/shard_map/all_to_all | solution.py:81
  44.9 0.8 fusion.98
  45.7 0.8 fusion.100
  46.5 0.8 fusion.74
  47.4 0.8 fusion.102
  48.2 0.2 multiply_bitcast_fusion.1
  48.4 0.1 copy.25
  48.5 1.2 multiply_bitcast_fusion
  49.7 0.1 copy.26
  49.8 20.1 %all-to-all-done = bf16[2,512,512]{2,0,1:T(2,128)(2,1)S(1)} async-done(((bf16[2,512,512]{2,0,1:T(2,128)(2,1)}), bf16[2,512,512]{2,0,1:T(2,128)(2,1)S(1)}, u32[]{:S(2)}, u32[]{:S(2)}) %all-to-all-start) | async-done | bytes 1048608 | tf_op jit(solution)/shard_map/all_to_all | solution.py:81
  69.9 0.8 copy.15
  70.7 0.3 copy.27
  71.0 0.0 slice-start
  71.0 5.9 %convolution_bitcast_fusion = f32[256,2048]{1,0:T(8,128)S(1)} fusion(bf16[256,2048]{1,0:T(8,128)(2,1)S(1)} %bitcast.77, bf16[2048,2048]{1,0:T(8,128)(2,1)} %copy-done.2), kind=kOutput, calls=%fused_computation.69 | convolution fusion | flops 2147483648 | bytes 11534336 | tf_op jit(solution)/shard_map/dot_general | solution.py:61
  76.9 0.0 slice-start.1
  76.9 5.9 %convolution_bitcast_fusion.1 = f32[256,2048]{1,0:T(8,128)S(1)} fusion(bf16[256,2048]{1,0:T(8,128)(2,1)S(1)} %bitcast.78, bf16[2048,2048]{1,0:T(8,128)(2,1)} %fusion.102), kind=kOutput, calls=%fused_computation.70 | convolution fusion | flops 2147483648 | bytes 11534336 | tf_op jit(solution)/shard_map/dot_general | solution.py:61
  82.8 1.2 fusion.16
  84.0 1.1 fusion.18
  85.2 2.4 %fusion.43 = f32[256,2048]{1,0:T(8,128)S(1)} fusion(bf16[2048,2048]{1,0:T(8,128)(2,1)S(1)} %bitcast.82, bf16[128,2048]{1,0:T(8,128)(2,1)S(1)} %fusion.18, bf16[128,2048]{1,0:T(8,128)(2,1)S(1)} %get-tuple-element.8), kind=kOutput, calls=%fused_computation.147 | convolution fusion | flops 2149580800 | bytes 11534336 | tf_op jit(solution)/shard_map/dot_general | solution.py:61
  87.6 5.7 %fusion.44 = f32[256,2048]{1,0:T(8,128)S(1)} fusion(bf16[2048,2048]{1,0:T(8,128)(2,1)} %fusion.102, bf16[128,2048]{1,0:T(8,128)(2,1)S(1)} %fusion.18, bf16[128,2048]{1,0:T(8,128)(2,1)S(1)} %get-tuple-element.8), kind=kOutput, calls=%fused_computation.148 | convolution fusion | flops 2149580800 | bytes 11534336 | tf_op jit(solution)/shard_map/dot_general | solution.py:61
  93.3 1.4 %fusion.20 = (bf16[128,2048]{1,0:T(8,128)(2,1)S(1)}, bf16[128,2048]{1,0:T(8,128)(2,1)S(1)}, bf16[128,2048]{1,0:T(8,128)(2,1)S(1)}) fusion(f32[128,2048]{1,0:T(8,128)S(1)} %bitcast.71, f32[256,2048]{1,0:T(8,128)S(1)} %fusion.44, f32[256,2048]{1,0:T(8,128)S(1)} %fusion.43), kind=kLoop, calls=%fused_computation.101 | loop fusion | flops 9961472 | bytes 6815744 | tf_op jit(solution)/shard_map/convert_element_type | solution.py:95
  94.7 1.1 fusion.22
  95.9 3.4 %fusion.6 = f32[256,512]{1,0:T(8,128)S(1)} fusion(s32[512]{0:T(512)S(1)} %broadcast_add_fusion.1, s32[2048]{0:T(1024)S(1)} %broadcast_add_fusion, bf16[128,2048]{1,0:T(8,128)(2,1)S(1)} %fusion.22, bf16[128,2048]{1,0:T(8,128)(2,1)S(1)} %get-tuple-element.5), kind=kOutput, calls=%fused_computation.71 | convolution fusion | flops 562036736 | bytes 1583104 | tf_op jit(solution)/shard_map/dot_general | solution.py:61
  99.3 5.0 %fusion.8 = f32[256,512]{1,0:T(8,128)S(1)} fusion(s32[512]{0:T(512)S(1)} %broadcast_add_fusion.1, s32[2048]{0:T(1024)S(1)} %broadcast_add_fusion, bf16[128,2048]{1,0:T(8,128)(2,1)S(1)} %fusion.22, bf16[128,2048]{1,0:T(8,128)(2,1)S(1)} %get-tuple-element.5), kind=kOutput, calls=%fused_computation.72 | convolution fusion | flops 576716800 | bytes 1583104 | tf_op jit(solution)/shard_map/dot_general | solution.py:61
  104.3 0.1 fusion.106
  104.5 0.1 copy.18
  104.6 0.1 copy.19
  104.7 0.7 copy.20
  105.5 3.7 %all-to-all-start.3 = ((bf16[32,2,16,128]{3,2,1,0:T(8,128)(2,1)}), bf16[32,2,16,128]{3,2,1,0:T(8,128)(2,1)S(1)}, u32[]{:S(2)}, u32[]{:S(2)}) async-start(bf16[32,2,16,128]{3,2,1,0:T(8,128)(2,1)} %copy.20), calls=%async_computation.3 | async-start | bytes 524288 | tf_op jit(solution)/shard_map/all_to_all | solution.py:107
  109.2 0.1 fusion.109
  109.3 10.1 %all-to-all-done.3 = bf16[32,2,16,128]{3,2,1,0:T(8,128)(2,1)S(1)} async-done(((bf16[32,2,16,128]{3,2,1,0:T(8,128)(2,1)}), bf16[32,2,16,128]{3,2,1,0:T(8,128)(2,1)S(1)}, u32[]{:S(2)}, u32[]{:S(2)}) %all-to-all-start.3) | async-done | bytes 262176 | tf_op jit(solution)/shard_map/all_to_all | solution.py:107
  119.4 0.3 fusion.108
  119.8 0.3 fusion.107
  120.1 0.3 convolution_subtract_fusion
  120.5 0.4 fusion.103
  120.9 0.4 fusion.137
  121.3 0.4 fusion.135
  121.7 0.4 fusion.14
  122.0 0.1 stack.21
  122.2 0.4 fusion.13
  122.6 0.1 stack.22
  122.7 0.7 maximum_multiply_fusion
  (32 shorter events, 0.7 us)
Async XLA Ops:
  2.8 20.8 %all-to-all-start.1 = ((bf16[4,128,512]{2,1,0:T(8,128)(2,1)}), bf16[4,128,512]{2,1,0:T(8,128)(2,1)S(1)}, u32[]{:S(2)}, u32[]{:S(2)}) async-start(bf16[4,128,512]{2,1,0:T(8,128)(2,1)} %bitcast.6), calls=%async_computation.1 | async-start | bytes 1048576 | tf_op jit(solution)/shard_map/all_to_all | solution.py:83
  11.3 7.3 %copy-start.2 = (bf16[2048,2048]{1,0:T(8,128)(2,1)}, bf16[2048,2048]{1,0:T(8,128)(2,1)S(1)}, u32[]{:S(2)}) copy-start(bf16[2048,2048]{1,0:T(8,128)(2,1)S(1)} %fusion.101) | copy-start | bytes 25165828
  13.6 13.6 %copy-start.1 = (bf16[2,512,512]{2,1,0:T(8,128)(2,1)S(1)}, bf16[2,512,512]{2,1,0:T(8,128)(2,1)}, u32[]{:S(2)}) copy-start(bf16[2,512,512]{2,1,0:T(8,128)(2,1)} %param.2) | copy-start | bytes 3145732
  23.6 17.5 %all-to-all-start.2 = ((bf16[4,128,512]{2,1,0:T(8,128)(2,1)}), bf16[4,128,512]{2,1,0:T(8,128)(2,1)S(1)}, u32[]{:S(2)}, u32[]{:S(2)}) async-start(bf16[4,128,512]{2,1,0:T(8,128)(2,1)} %bitcast.8), calls=%async_computation.2 | async-start | bytes 1048576 | tf_op jit(solution)/shard_map/all_to_all | solution.py:83
  41.1 7.1 %copy-start = (bf16[4,128,512]{2,1,0:T(8,128)(2,1)}, bf16[4,128,512]{2,1,0:T(8,128)(2,1)S(1)}, u32[]{:S(2)}) copy-start(bf16[4,128,512]{2,1,0:T(8,128)(2,1)S(1)} %all-to-all-done.2) | copy-start | bytes 1572868
  41.1 28.8 %all-to-all-start = ((bf16[2,512,512]{2,0,1:T(2,128)(2,1)}), bf16[2,512,512]{2,0,1:T(2,128)(2,1)S(1)}, u32[]{:S(2)}, u32[]{:S(2)}) async-start(bf16[2,512,512]{2,0,1:T(2,128)(2,1)} %copy.14), calls=%async_computation | async-start | bytes 2097152 | tf_op jit(solution)/shard_map/all_to_all | solution.py:81
  71.0 14.2 %slice-start = ((s8[8388608]{0:T(1024)(128)(4,1)}), s8[4194304]{0:T(1024)(128)(4,1)S(1)}, s32[]{:S(2)}) async-start(s8[8388608]{0:T(1024)(128)(4,1)} %bitcast.81), calls=%async_computation.4 | async-start | bytes 8388608
  76.9 8.3 %slice-start.1 = ((s8[8388608]{0:T(1024)(128)(4,1)}), s8[4194304]{0:T(1024)(128)(4,1)S(1)}, s32[]{:S(2)}) async-start(s8[8388608]{0:T(1024)(128)(4,1)} %bitcast.81), calls=%async_computation.5 | async-start | bytes 8388608
  105.5 13.9 %all-to-all-start.3 = ((bf16[32,2,16,128]{3,2,1,0:T(8,128)(2,1)}), bf16[32,2,16,128]{3,2,1,0:T(8,128)(2,1)S(1)}, u32[]{:S(2)}, u32[]{:S(2)}) async-start(bf16[32,2,16,128]{3,2,1,0:T(8,128)(2,1)} %copy.20), calls=%async_computation.3 | async-start | bytes 524288 | tf_op jit(solution)/shard_map/all_to_all | solution.py:107

commit v2 on v1

--- a/solution.py
+++ b/solution.py
@@ -3,6 +3,8 @@
 import jax
 import jax.numpy as jnp
 from jax import lax
+from jax.experimental import pallas as pl
+from jax.experimental.pallas import tpu as pltpu
 from jax.sharding import PartitionSpec as P
 
 AV = 512
@@ -39,7 +41,7 @@
 
 
 def propagator(points):
-    band = math.gcd(points, 128)
+    band = math.gcd(points, 256)
     offset = count(points)[None, :] - count(band)[:, None]
     cos, sin = unit_angle(offset * offset - points // 4, 2 * points)
     gain = 1.0 / math.sqrt(points)
@@ -66,6 +68,70 @@
     with_cos = matmul(both, table_cos)
     with_sin = matmul(both, table_sin)
     return with_cos[:rows] - with_sin[rows:], with_sin[:rows] + with_cos[rows:]
+
+
+def exchange_kernel(groups, devices, source, target, send_sem, recv_sem, own_sem):
+    me = lax.axis_index("slab") * groups + lax.axis_index("grp")
+    barrier = pltpu.get_barrier_semaphore()
+
+    def place(device):
+        return (lax.div(device, groups), lax.rem(device, groups))
+
+    def greet(step, carry):
+        peer = lax.rem(me + step, devices)
+        pl.semaphore_signal(
+            barrier, inc=1, device_id=place(peer), device_id_type=pl.DeviceIdType.MESH
+        )
+        return carry
+
+    lax.fori_loop(1, devices, greet, 0)
+    pl.semaphore_wait(barrier, devices - 1)
+
+    def block(step):
+        peer = lax.rem(me + step, devices)
+        return pltpu.make_async_remote_copy(
+            src_ref=source.at[peer],
+            dst_ref=target.at[me],
+            send_sem=send_sem.at[step],
+            recv_sem=recv_sem.at[step],
+            device_id=place(peer),
+            device_id_type=pl.DeviceIdType.MESH,
+        )
+
+    def send(step, carry):
+        block(step).start()
+        return carry
+
+    def wait(step, carry):
+        block(step).wait()
+        return carry
+
+    lax.fori_loop(1, devices, send, 0)
+    own = pltpu.make_async_copy(source.at[me], target.at[me], own_sem)
+    own.start()
+    own.wait()
+    lax.fori_loop(1, devices, wait, 0)
+
+
+def exchange(blocks, groups):
+    devices = blocks.shape[0]
+
+    def kernel(*refs):
+        exchange_kernel(groups, devices, *refs)
+
+    return pl.pallas_call(
+        kernel,
+        out_shape=jax.ShapeDtypeStruct(blocks.shape, blocks.dtype),
+        in_specs=[pl.BlockSpec(memory_space=pltpu.VMEM)],
+        out_specs=pl.BlockSpec(memory_space=pltpu.VMEM),
+        scratch_shapes=[
+            pltpu.SemaphoreType.DMA((devices,)),
+            pltpu.SemaphoreType.DMA((devices,)),
+            pltpu.SemaphoreType.DMA,
+        ],
+        compiler_params=pltpu.CompilerParams(collective_id=0, has_side_effects=True),
+        name="column_exchange",
+    )(blocks)
 
 
 def on_device(near_field, lens_phase):
@@ -79,9 +145,17 @@
     angles = AV // devices
     coded = [jnp.exp2(lens_phase[k] * PHASE_CODE).astype(jnp.bfloat16) for k in range(steps)]
     field = lax.all_to_all(near_field, "grp", split_axis=1, concat_axis=2, tiled=True)
-    coded = [
-        lax.all_to_all(part, "grp", split_axis=0, concat_axis=1, tiled=True) for part in coded
-    ]
+    arrived = field
+    moved = []
+    for part in coded:
+        part, arrived = lax.optimization_barrier((part, arrived))
+        if not moved:
+            field = arrived
+        else:
+            moved[-1] = arrived
+        arrived = lax.all_to_all(part, "grp", split_axis=0, concat_axis=1, tiled=True)
+        moved.append(arrived)
+    coded = moved
     prop_cos, prop_sin = propagator(points)
     both = field.reshape(2 * rows, points)
     for section in range(steps):
@@ -101,10 +175,12 @@
         count(AV) - AV // 2,
         2 * points,
     )
-    col_real, col_imag = complex_product(both, vert_cos, -vert_sin)
+    vert_cos, vert_sin = lax.optimization_barrier((vert_cos, -vert_sin))
+    col_real, col_imag = complex_product(both, vert_cos, vert_sin)
     cols = jnp.stack([col_real, col_imag]).astype(jnp.bfloat16)
     cols = jnp.transpose(cols.reshape(2, rows, devices, angles), (2, 0, 3, 1))
-    got = lax.all_to_all(cols, ("slab", "grp"), split_axis=0, concat_axis=0, tiled=True)
+    got = exchange(cols.reshape(devices, 2 * angles, rows), group_count)
+    got = got.reshape(devices, 2, angles, rows)
     modulus = 2 * total_rows
     period = modulus // rows
     source = count(devices) - devices // 2

time: 124 us -> 102 us (0.82)
  waiting for transfers between devices: 43.7 us -> 4.58 us
  Pallas kernels: 0 us -> 15 us
  local copies, waits for them, and re-layouts: 5.58 us -> 16.6 us
  matrix products: 31.3 us -> 27.2 us
  starting transfers between devices: 17.2 us -> 14.1 us
  other arithmetic: 25.2 us -> 23.2 us
    all_to_all x1, waiting for transfers between devices: 20.1 us -> 3.78 us  [on_device(): lax.all_to_all(near_field, 'grp', split_axis=1, concat_axis=2, tiled=True)]
    pallas_call x0 -> x1, Pallas kernels: none -> 15 us  [exchange(): pl.pallas_call(kernel, out_shape=jax.ShapeDtypeStruct(blocks.shape, block...]
    unnamed x31 -> x14, other arithmetic: 14.3 us -> 1.07 us
    all_to_all x2, waiting for transfers between devices: 13.5 us -> 0.79 us  [on_device(): lax.all_to_all(part, 'grp', split_axis=0, concat_axis=1, tiled=True)]
    all_to_all x1 -> x0, waiting for transfers between devices: 10.1 us -> none  [on_device(): lax.all_to_all(cols, ('slab', 'grp'), split_axis=0, concat_axis=0, tiled=...]
    unnamed x14 -> x21, local copies, waits for them, and re-layouts: 3.35 us -> 12 us
    neg x0 -> x1, other arithmetic: none -> 6.11 us  [on_device(): vert_cos, vert_sin = lax.optimization_barrier((vert_cos, -vert_sin))]
    convert_element_type x0 -> x1, other arithmetic: none -> 4.25 us  [phase_table(): return (cos.astype(jnp.bfloat16), sin.astype(jnp.bfloat16))]
  transfers between devices with their start and end apart: 4 -> 3, of which waited for: 4 -> 2; matrix products, arithmetic and copies ran while one was open for 16% -> 42% of each run, Pallas kernels for 0% -> 0%
where the time goes in v2:
time: 102 us; the launch traced here: 101 us
  matrix products  27.2 us (27%)
  other arithmetic  23.2 us (23%)
  local copies, waits for them, and re-layouts  16.6 us (16%)
  Pallas kernels  15 us (15%)
  starting transfers between devices  14.1 us (14%)
  waiting for transfers between devices  4.58 us (4%)
    dot_general x6, matrix products, matmul(): return jnp.dot(left, right, preferred_element_type=jnp.float32)  24.3 us
    pallas_call x1, Pallas kernels, exchange(): pl.pallas_call(kernel, out_shape=jax.ShapeDtypeStruct(blocks.shape, block...  15 us
    unnamed x21, local copies, waits for them, and re-layouts  12 us
    all_to_all x2, starting transfers between devices, on_device(): lax.all_to_all(part, 'grp', split_axis=0, concat_axis=1, tiled=True)  7.75 us
    all_to_all x1, starting transfers between devices, on_device(): lax.all_to_all(near_field, 'grp', split_axis=1, concat_axis=2, tiled=True)  6.35 us
    neg x1, other arithmetic, on_device(): vert_cos, vert_sin = lax.optimization_barrier((vert_cos, -vert_sin))  6.11 us
    convert_element_type x1, other arithmetic, phase_table(): return (cos.astype(jnp.bfloat16), sin.astype(jnp.bfloat16))  4.25 us
    convert_element_type x2, other arithmetic, on_device(): (real * lens_cos - imag * lens_sin).astype(jnp.bfloat16)  4.09 us
  transfers between devices with their start and end apart: 3, of which 2 were waited for; matrix products, arithmetic and copies ran while one was open for 42% of the time, Pallas kernels for 0%

profile of v2, /device:TPU:0, one launch (start us, length us, event | category | flops | bytes accessed | tf_op | source)
XLA Modules:
  0.0 101.1 jit_solution(7343262945690920122)
XLA Ops:
  0.0 3.3 %copy.25 = bf16[2,512,512]{2,0,1:T(2,128)(2,1)} copy(bf16[2,512,512]{2,1,0:T(8,128)(2,1)} %param.2) | data formatting | bytes 2097152 | tf_op args[0]
  3.3 6.3 %all-to-all-start = ((bf16[2,512,512]{2,0,1:T(2,128)(2,1)}), bf16[2,512,512]{2,0,1:T(2,128)(2,1)S(1)}, u32[]{:S(2)}, u32[]{:S(2)}) async-start(bf16[2,512,512]{2,0,1:T(2,128)(2,1)} %copy.25), calls=%async_computation | async-start | bytes 2097152 | tf_op jit(solution)/shard_map/all_to_all | solution.py:147
  9.7 4.2 %fusion.1 = bf16[2048,512]{1,0:T(8,128)(2,1)} fusion(s32[512]{0:T(512)S(1)} %broadcast_add_fusion.1, s32[2048]{0:T(1024)S(1)} %broadcast_add_fusion), kind=kLoop, calls=%fused_computation.3 | loop fusion | flops 23068672 | bytes 2107392 | tf_op jit(solution)/shard_map/convert_element_type | solution.py:40
  13.9 6.1 %fusion.11 = bf16[2048,512]{1,0:T(8,128)(2,1)} fusion(s32[512]{0:T(512)S(1)} %broadcast_add_fusion.1, s32[2048]{0:T(1024)S(1)} %broadcast_add_fusion), kind=kLoop, calls=%fused_computation.44 | loop fusion | flops 37748736 | bytes 2107392 | tf_op jit(solution)/shard_map/neg | solution.py:178
  20.0 2.8 %fusion.10 = (bf16[256,2048]{1,0:T(8,128)(2,1)S(1)}, bf16[256,2048]{1,0:T(8,128)(2,1)S(1)}) fusion(s32[256]{0:T(256)S(1)} %iota.24, s32[2048]{0:T(1024)S(1)} %iota.23), kind=kLoop, calls=%fused_computation.43 | loop fusion | flops 20447232 | bytes 2106368 | tf_op jit(solution)/shard_map/convert_element_type | solution.py:50
  22.8 0.1 constant_dynamic-update-slice_fusion.1
  22.9 0.1 fusion.30
  23.0 0.1 fusion.32
  23.1 0.1 fusion.34
  23.2 0.1 fusion.36
  23.3 0.1 fusion.38
  23.3 0.1 fusion.28
  23.4 0.1 fusion.55
  23.5 0.1 constant_dynamic-update-slice_fusion
  23.6 0.1 fusion.42
  23.8 0.1 fusion.44
  23.9 0.1 fusion.75
  24.0 0.1 fusion.46
  24.1 0.1 fusion.48
  24.1 2.6 %copy-done.5 = bf16[2048,2048]{1,0:T(8,128)(2,1)} copy-done((bf16[2048,2048]{1,0:T(8,128)(2,1)}, bf16[2048,2048]{1,0:T(8,128)(2,1)S(1)}, u32[]{:S(2)}) %copy-start.5) | copy-done | bytes 8388632
  26.8 0.1 fusion.50
  26.8 0.1 fusion.40
  26.9 0.1 fusion.56
  27.0 3.3 %copy-done.6 = bf16[2048,2048]{1,0:T(8,128)(2,1)} copy-done((bf16[2048,2048]{1,0:T(8,128)(2,1)}, bf16[2048,2048]{1,0:T(8,128)(2,1)S(1)}, u32[]{:S(2)}) %copy-start.6) | copy-done | bytes 8388632
  30.3 1.3 %fusion.67 = (bf16[512,512]{1,0:T(8,128)(2,1)}, bf16[512,512]{1,0:T(8,128)(2,1)}) fusion(f32[2,512,512]{2,1,0:T(8,128)S(1)} %copy-done), kind=kLoop, calls=%fused_computation.141 | loop fusion | flops 1048576 | bytes 3145728 | tf_op jit(solution)/shard_map/convert_element_type | solution.py:146
  31.6 3.8 %all-to-all-done = bf16[2,512,512]{2,0,1:T(2,128)(2,1)S(1)} async-done(((bf16[2,512,512]{2,0,1:T(2,128)(2,1)}), bf16[2,512,512]{2,0,1:T(2,128)(2,1)S(1)}, u32[]{:S(2)}, u32[]{:S(2)}) %all-to-all-start) | async-done | bytes 1048608 | tf_op jit(solution)/shard_map/all_to_all | solution.py:147
  35.4 0.2 copy.26
  35.5 0.7 copy.27
  36.2 1.3 %copy.28 = bf16[2,128,2048]{2,1,0:T(8,128)(2,1)} copy(bf16[2,128,2048]{1,2,0:T(8,128)(2,1)S(1)} %bitcast.79) | data formatting | bytes 2097152 | tf_op jit(solution)/shard_map/optimization_barrier | solution.py:151
  37.5 3.5 %all-to-all-start.1 = ((bf16[4,128,512]{2,1,0:T(8,128)(2,1)}), bf16[4,128,512]{2,1,0:T(8,128)(2,1)S(1)}, u32[]{:S(2)}, u32[]{:S(2)}) async-start(bf16[4,128,512]{2,1,0:T(8,128)(2,1)} %bitcast.8), calls=%async_computation.1 | async-start | bytes 1048576 | tf_op jit(solution)/shard_map/all_to_all | solution.py:156
  41.0 6.1 %fusion.231 = f32[256,2048]{1,0:T(8,128)S(1)} fusion(bf16[256,2048]{1,0:T(8,128)(2,1)} %bitcast.82, bf16[2048,2048]{1,0:T(8,128)(2,1)} %copy-done.5), kind=kOutput, calls=%fused_computation.326 | convolution fusion | flops 2147483648 | bytes 11534336 | tf_op jit(solution)/shard_map/dot_general | solution.py:63
  47.2 7.1 %fusion.230 = f32[256,2048]{1,0:T(8,128)} fusion(bf16[256,2048]{1,0:T(8,128)(2,1)S(1)} %bitcast.83, bf16[2048,2048]{1,0:T(8,128)(2,1)} %copy-done.6), kind=kOutput, calls=%fused_computation.325 | convolution fusion | flops 2147483648 | bytes 11534336 | tf_op jit(solution)/shard_map/dot_general | solution.py:63
  54.2 0.8 all-to-all-done.1
  55.1 4.3 %all-to-all-start.2 = ((bf16[4,128,512]{2,1,0:T(8,128)(2,1)}), bf16[4,128,512]{2,1,0:T(8,128)(2,1)S(1)}, u32[]{:S(2)}, u32[]{:S(2)}) async-start(bf16[4,128,512]{2,1,0:T(8,128)(2,1)} %bitcast.81), calls=%async_computation.2 | async-start | bytes 1048576 | tf_op jit(solution)/shard_map/all_to_all | solution.py:156
  59.4 2.9 %fusion.18 = (bf16[128,2048]{1,0:T(8,128)(2,1)S(1)}, bf16[128,2048]{1,0:T(8,128)(2,1)S(1)}, bf16[128,2048]{1,0:T(8,128)(2,1)S(1)}) fusion(bf16[128,2048]{1,0:T(8,128)(2,1)S(1)} %bitcast.76, f32[256,2048]{1,0:T(8,128)} %fusion.230, f32[256,2048]{1,0:T(8,128)S(1)} %fusion.231), kind=kLoop, calls=%fused_computation.72 | loop fusion | flops 10485760 | bytes 6291456 | tf_op jit(solution)/shard_map/convert_element_type | solution.py:169
  62.3 1.3 %fusion.20 = bf16[128,2048]{1,0:T(8,128)(2,1)S(1)} fusion(bf16[128,2048]{1,0:T(8,128)(2,1)S(1)} %get-tuple-element.22, bf16[128,2048]{1,0:T(8,128)(2,1)S(1)} %get-tuple-element.21, bf16[128,2048]{1,0:T(8,128)(2,1)S(1)} %bitcast.77), kind=kLoop, calls=%fused_computation.74 | loop fusion | flops 9437184 | bytes 2097152 | tf_op jit(solution)/shard_map/convert_element_type | solution.py:170
  63.6 5.9 %fusion.65 = f32[256,2048]{1,0:T(8,128)S(1)} fusion(bf16[2048,2048]{1,0:T(8,128)(2,1)} %copy-done.5, bf16[128,2048]{1,0:T(8,128)(2,1)S(1)} %fusion.20, bf16[128,2048]{1,0:T(8,128)(2,1)S(1)} %get-tuple-element.20), kind=kOutput, calls=%fused_computation.139 | convolution fusion | flops 2149580800 | bytes 11534336 | tf_op jit(solution)/shard_map/dot_general | solution.py:63
  69.5 3.8 %fusion.66 = f32[256,2048]{1,0:T(8,128)} fusion(bf16[2048,2048]{1,0:T(8,128)(2,1)S(1)} %bitcast.89, bf16[128,2048]{1,0:T(8,128)(2,1)S(1)} %fusion.20, bf16[128,2048]{1,0:T(8,128)(2,1)S(1)} %get-tuple-element.20), kind=kOutput, calls=%fused_computation.140 | convolution fusion | flops 2149580800 | bytes 11534336 | tf_op jit(solution)/shard_map/dot_general | solution.py:63
  73.3 0.2 multiply_bitcast_fusion
  73.4 0.1 copy.39
  73.5 1.3 %copy-done.3 = f32[256,2048]{1,0:T(8,128)S(1)} copy-done((f32[256,2048]{1,0:T(8,128)S(1)}, f32[256,2048]{1,0:T(8,128)}, u32[]{:S(2)}) %copy-start.3) | copy-done | bytes 2097176
  74.9 1.2 %fusion.22 = (bf16[128,2048]{1,0:T(8,128)(2,1)S(1)}, bf16[128,2048]{1,0:T(8,128)(2,1)S(1)}, bf16[128,2048]{1,0:T(8,128)(2,1)S(1)}) fusion(f32[128,2048]{1,0:T(8,128)S(1)} %bitcast.74, f32[256,2048]{1,0:T(8,128)S(1)} %copy-done.3, f32[256,2048]{1,0:T(8,128)S(1)} %fusion.65), kind=kLoop, calls=%fused_computation.76 | loop fusion | flops 9961472 | bytes 6815744 | tf_op jit(solution)/shard_map/convert_element_type | solution.py:169
  76.1 1.1 %fusion.24 = bf16[128,2048]{1,0:T(8,128)(2,1)S(1)} fusion(bf16[128,2048]{1,0:T(8,128)(2,1)S(1)} %get-tuple-element.19, bf16[128,2048]{1,0:T(8,128)(2,1)S(1)} %get-tuple-element.18, f32[128,2048]{1,0:T(8,128)S(1)} %bitcast.75), kind=kLoop, calls=%fused_computation.78 | loop fusion | flops 8912896 | bytes 2621440 | tf_op jit(solution)/shard_map/convert_element_type | solution.py:170
  77.2 0.4 copy-done.2
  77.6 0.7 fusion.64
  78.4 0.9 copy-done.1
  79.2 0.7 fusion.63
  80.0 0.1 fusion.72
  80.1 0.1 copy.31
  80.2 0.1 copy.32
  80.4 0.7 copy.33
  81.1 15.0 %column_exchange.1 = bf16[32,32,128]{2,1,0:T(8,128)(2,1)} custom-call(bf16[32,32,128]{2,1,0:T(8,128)(2,1)} %bitcast.85), custom_call_target="tpu_custom_call" | custom-call | tf_op jit(solution)/shard_map/column_exchange/pallas_call | solution.py:122
  96.1 1.0 fusion.227
  97.1 0.3 fusion.74
  97.4 0.3 fusion.73
  97.8 0.3 convolution_subtract_fusion
  98.1 0.4 fusion.69
  98.6 0.4 fusion.103
  98.9 0.4 fusion.101
  99.3 0.4 fusion.16
  99.7 0.1 stack.21
  99.8 0.4 fusion.15
  100.2 0.1 stack.22
  100.3 0.7 maximum_multiply_fusion
  (26 shorter events, 0.1 us)
Async XLA Ops:
  3.3 32.1 %all-to-all-start = ((bf16[2,512,512]{2,0,1:T(2,128)(2,1)}), bf16[2,512,512]{2,0,1:T(2,128)(2,1)S(1)}, u32[]{:S(2)}, u32[]{:S(2)}) async-start(bf16[2,512,512]{2,0,1:T(2,128)(2,1)} %copy.25), calls=%async_computation | async-start | bytes 2097152 | tf_op jit(solution)/shard_map/all_to_all | solution.py:147
  23.5 3.2 %copy-start.5 = (bf16[2048,2048]{1,0:T(8,128)(2,1)}, bf16[2048,2048]{1,0:T(8,128)(2,1)S(1)}, u32[]{:S(2)}) copy-start(bf16[2048,2048]{1,0:T(8,128)(2,1)S(1)} %fusion.55) | copy-start | bytes 25165828
  26.8 3.5 %copy-start = (f32[2,512,512]{2,1,0:T(8,128)S(1)}, f32[2,512,512]{2,1,0:T(8,128)}, u32[]{:S(2)}) copy-start(f32[2,512,512]{2,1,0:T(8,128)} %param.3) | copy-start | bytes 6291460
  27.0 3.3 %copy-start.6 = (bf16[2048,2048]{1,0:T(8,128)(2,1)}, bf16[2048,2048]{1,0:T(8,128)(2,1)S(1)}, u32[]{:S(2)}) copy-start(bf16[2048,2048]{1,0:T(8,128)(2,1)S(1)} %fusion.56) | copy-start | bytes 25165828
  37.5 17.5 %all-to-all-start.1 = ((bf16[4,128,512]{2,1,0:T(8,128)(2,1)}), bf16[4,128,512]{2,1,0:T(8,128)(2,1)S(1)}, u32[]{:S(2)}, u32[]{:S(2)}) async-start(bf16[4,128,512]{2,1,0:T(8,128)(2,1)} %bitcast.8), calls=%async_computation.1 | async-start | bytes 1048576 | tf_op jit(solution)/shard_map/all_to_all | solution.py:156
  41.0 6.1 %copy-start.4 = (bf16[2,128,2048]{2,1,0:T(8,128)(2,1)S(1)}, bf16[2,128,2048]{2,1,0:T(8,128)(2,1)}, u32[]{:S(2)}) copy-start(bf16[2,128,2048]{2,1,0:T(8,128)(2,1)} %copy.28) | copy-start | bytes 3145732
  55.1 18.2 %all-to-all-start.2 = ((bf16[4,128,512]{2,1,0:T(8,128)(2,1)}), bf16[4,128,512]{2,1,0:T(8,128)(2,1)S(1)}, u32[]{:S(2)}, u32[]{:S(2)}) async-start(bf16[4,128,512]{2,1,0:T(8,128)(2,1)} %bitcast.81), calls=%async_computation.2 | async-start | bytes 1048576 | tf_op jit(solution)/shard_map/all_to_all | solution.py:156
  62.3 7.2 %slice-start = ((s8[8388608]{0:T(1024)(128)(4,1)}), s8[4194304]{0:T(1024)(128)(4,1)S(1)}, s32[]{:S(2)}) async-start(s8[8388608]{0:T(1024)(128)(4,1)} %bitcast.88), calls=%async_computation.3 | async-start | bytes 8388608
  63.6 5.9 %slice-start.1 = ((s8[8388608]{0:T(1024)(128)(4,1)}), s8[4194304]{0:T(1024)(128)(4,1)S(1)}, s32[]{:S(2)}) async-start(s8[8388608]{0:T(1024)(128)(4,1)} %bitcast.88), calls=%async_computation.4 | async-start | bytes 8388608
  73.3 1.6 %copy-start.3 = (f32[256,2048]{1,0:T(8,128)S(1)}, f32[256,2048]{1,0:T(8,128)}, u32[]{:S(2)}) copy-start(f32[256,2048]{1,0:T(8,128)} %fusion.66) | copy-start | bytes 6291460
  76.0 1.6 %copy-start.2 = (bf16[2048,512]{1,0:T(8,128)(2,1)S(1)}, bf16[2048,512]{1,0:T(8,128)(2,1)}, u32[]{:S(2)}) copy-start(bf16[2048,512]{1,0:T(8,128)(2,1)} %fusion.1) | copy-start | bytes 6291460
  77.6 1.6 %copy-start.1 = (bf16[2048,512]{1,0:T(8,128)(2,1)S(1)}, bf16[2048,512]{1,0:T(8,128)(2,1)}, u32[]{:S(2)}) copy-start(bf16[2048,512]{1,0:T(8,128)(2,1)} %fusion.11) | copy-start | bytes 6291460

commit v3 on v2

--- a/solution.py
+++ b/solution.py
@@ -38,6 +38,11 @@
 def phase_table(row_index, col_index, modulus):
     cos, sin = unit_angle(row_index[:, None] * col_index[None, :], modulus)
     return cos.astype(jnp.bfloat16), sin.astype(jnp.bfloat16)
+
+
+def conjugate(table):
+    cos, sin = table
+    return jnp.stack([jnp.stack([cos, -sin]), jnp.stack([sin, cos])])
 
 
 def propagator(points):
@@ -144,7 +149,8 @@
     rows = lat_dev // group_count
     angles = AV // devices
     coded = [jnp.exp2(lens_phase[k] * PHASE_CODE).astype(jnp.bfloat16) for k in range(steps)]
-    field = lax.all_to_all(near_field, "grp", split_axis=1, concat_axis=2, tiled=True)
+    blocks = jnp.transpose(near_field.reshape(2, group_count, rows, width), (1, 0, 2, 3))
+    field = lax.all_to_all(blocks, "grp", split_axis=0, concat_axis=0, tiled=True)
     arrived = field
     moved = []
     for part in coded:
@@ -157,7 +163,7 @@
         moved.append(arrived)
     coded = moved
     prop_cos, prop_sin = propagator(points)
-    both = field.reshape(2 * rows, points)
+    both = jnp.transpose(field, (1, 2, 0, 3)).reshape(2 * rows, points)
     for section in range(steps):
         real, imag = complex_product(both, prop_cos, prop_sin)
         real = real.astype(jnp.bfloat16).astype(jnp.float32)
@@ -171,36 +177,34 @@
             ]
         )
     vert_cos, vert_sin = phase_table(
-        count(points) - points // 2,
-        count(AV) - AV // 2,
-        2 * points,
+        count(AV) - AV // 2, count(points) - points // 2, 2 * points
     )
-    vert_cos, vert_sin = lax.optimization_barrier((vert_cos, -vert_sin))
-    col_real, col_imag = complex_product(both, vert_cos, vert_sin)
-    cols = jnp.stack([col_real, col_imag]).astype(jnp.bfloat16)
-    cols = jnp.transpose(cols.reshape(2, rows, devices, angles), (2, 0, 3, 1))
+    vert_cos, vert_sin = lax.optimization_barrier((vert_cos, vert_sin))
+    with_cos = jnp.einsum("av,nv->an", vert_cos, both, preferred_element_type=jnp.float32)
+    with_sin = jnp.einsum("av,nv->an", vert_sin, both, preferred_element_type=jnp.float32)
+    col_real = (with_cos[:, :rows] + with_sin[:, rows:]).astype(jnp.bfloat16)
+    col_imag = (with_cos[:, rows:] - with_sin[:, :rows]).astype(jnp.bfloat16)
+    cols = jnp.stack([part.reshape(devices, angles, rows) for part in (col_real, col_imag)], axis=1)
     got = exchange(cols.reshape(devices, 2 * angles, rows), group_count)
-    got = got.reshape(devices, 2, angles, rows)
     modulus = 2 * total_rows
     period = modulus // rows
     source = count(devices) - devices // 2
     fine = count(period)
     near = count(rows)
     coarse = count(AL // period)
-    w_cos, w_sin = phase_table(source, fine, period)
-    got_real = got[:, 0]
-    got_imag = got[:, 1]
-    ein = lambda s, l, r: jnp.einsum(s, l, r, preferred_element_type=jnp.float32)
-    mid_real = ein("sam,sf->afm", got_real, w_cos) + ein("sam,sf->afm", got_imag, w_sin)
-    mid_imag = ein("sam,sf->afm", got_imag, w_cos) - ein("sam,sf->afm", got_real, w_sin)
+    scale = 1.0 / math.sqrt(total_rows * points)
+    got = got.reshape(devices, 2, angles, rows)
+    weights = conjugate(phase_table(source, fine, period))
+    mid = jnp.einsum("skam,kcsf->cafm", got, weights, preferred_element_type=jnp.float32)
     t_cos, t_sin = unit_angle(fine[:, None] * near[None, :], modulus)
-    turned_real = (mid_real * t_cos + mid_imag * t_sin).astype(jnp.bfloat16)
-    turned_imag = (mid_imag * t_cos - mid_real * t_sin).astype(jnp.bfloat16)
-    e_cos, e_sin = phase_table(near, coarse * period - AL // 2, modulus)
-    out_real = ein("afm,mc->acf", turned_real, e_cos) + ein("afm,mc->acf", turned_imag, e_sin)
-    out_imag = ein("afm,mc->acf", turned_imag, e_cos) - ein("afm,mc->acf", turned_real, e_sin)
-    scale = 1.0 / math.sqrt(total_rows * points)
-    return (jnp.stack([out_real, out_imag]) * scale).reshape(2, angles, AL)
+    t_cos = t_cos * scale
+    t_sin = t_sin * scale
+    turned = jnp.stack([mid[0] * t_cos + mid[1] * t_sin, mid[1] * t_cos - mid[0] * t_sin])
+    weights = conjugate(phase_table(near, coarse * period - AL // 2, modulus))
+    out = jnp.einsum(
+        "kafm,kcmd->cadf", turned.astype(jnp.bfloat16), weights, preferred_element_type=jnp.float32
+    )
+    return out.reshape(2, angles, AL)
 
 
 def solution(mesh):

time: 102 us -> 98 us (0.961)
  waiting for transfers between devices: 4.58 us -> 10.7 us
  local copies, waits for them, and re-layouts: 16.6 us -> 11.6 us
  other arithmetic: 23.2 us -> 19.7 us
  matrix products: 27.2 us -> 26 us
    all_to_all x1, waiting for transfers between devices: 3.78 us -> 9.93 us  [on_device(): lax.all_to_all(blocks, 'grp', split_axis=0, concat_axis=0, tiled=True)]
    neg x1 -> x2, other arithmetic: 6.11 us -> 0.2 us  [conjugate(): return jnp.stack([jnp.stack([cos, -sin]), jnp.stack([sin, cos])])]
    unnamed x21, local copies, waits for them, and re-layouts: 12 us -> 7.4 us
    transpose x1 -> x2, local copies, waits for them, and re-layouts: 0.72 us -> 3.12 us  [the longest x1 2.3 us: on_device(): jnp.transpose(near_field.reshape(2, group_count, rows, width), (1, 0, 2, 3))]
    convert_element_type x1 -> x3, other arithmetic: 4.25 us -> 6.51 us  [phase_table(): return (cos.astype(jnp.bfloat16), sin.astype(jnp.bfloat16))]
    dot_general x6 -> x4, matrix products: 24.3 us -> 22.9 us  [matmul(): return jnp.dot(left, right, preferred_element_type=jnp.float32)]
    optimization_barrier x1 -> x0, local copies, waits for them, and re-layouts: 1.32 us -> none  [on_device(): part, arrived = lax.optimization_barrier((part, arrived))]
    dot_general x8 -> x4, matrix products: 2.95 us -> 3.14 us  [the longest x1 1.27 us: on_device(): jnp.einsum('skam,kcsf->cafm', got, weights, preferred_element_type=jnp.fl...]
  transfers between devices with their start and end apart: 3 -> 3, of which waited for: 2 -> 2; matrix products, arithmetic and copies ran while one was open for 42% -> 40% of each run, Pallas kernels for 0% -> 0%
where the time goes in v3:
time: 98 us; the launch traced here: 97.4 us
  matrix products  26 us (27%)
  other arithmetic  19.7 us (20%)
  Pallas kernels  15 us (15%)
  starting transfers between devices  14.1 us (14%)
  local copies, waits for them, and re-layouts  11.6 us (12%)
  waiting for transfers between devices  10.7 us (11%)
    dot_general x4, matrix products, matmul(): return jnp.dot(left, right, preferred_element_type=jnp.float32)  22.9 us
    pallas_call x1, Pallas kernels, exchange(): pl.pallas_call(kernel, out_shape=jax.ShapeDtypeStruct(blocks.shape, block...  15 us
    all_to_all x1, waiting for transfers between devices, on_device(): lax.all_to_all(blocks, 'grp', split_axis=0, concat_axis=0, tiled=True)  9.93 us
    all_to_all x2, starting transfers between devices, on_device(): lax.all_to_all(part, 'grp', split_axis=0, concat_axis=1, tiled=True)  7.76 us
    unnamed x21, local copies, waits for them, and re-layouts  7.4 us
    convert_element_type x3, other arithmetic, phase_table(): return (cos.astype(jnp.bfloat16), sin.astype(jnp.bfloat16))  6.51 us
    all_to_all x1, starting transfers between devices, on_device(): lax.all_to_all(blocks, 'grp', split_axis=0, concat_axis=0, tiled=True)  6.35 us
    convert_element_type x2, other arithmetic, on_device(): (real * lens_cos - imag * lens_sin).astype(jnp.bfloat16)  4.09 us
  transfers between devices with their start and end apart: 3, of which 2 were waited for; matrix products, arithmetic and copies ran while one was open for 40% of the time, Pallas kernels for 0%

profile of v3, /device:TPU:0, one launch (start us, length us, event | category | flops | bytes accessed | tf_op | source)
XLA Modules:
  0.0 97.4 jit_solution(8805766602201569634)
XLA Ops:
  0.0 2.3 %copy.31 = bf16[4,2,128,512]{3,2,1,0:T(8,128)(2,1)} copy(bf16[4,2,128,512]{3,2,0,1:T(8,128)(2,1)} %bitcast.84) | data formatting | bytes 2097152 | tf_op jit(solution)/shard_map/transpose | solution.py:152
  2.3 6.3 %all-to-all-start = ((bf16[4,2,128,512]{3,2,1,0:T(8,128)(2,1)}), bf16[4,2,128,512]{3,2,1,0:T(8,128)(2,1)S(1)}, u32[]{:S(2)}, u32[]{:S(2)}) async-start(bf16[4,2,128,512]{3,2,1,0:T(8,128)(2,1)} %copy.31), calls=%async_computation | async-start | bytes 2097152 | tf_op jit(solution)/shard_map/all_to_all | solution.py:153
  8.7 0.1 fusion.87
  8.8 0.1 fusion.94
  8.9 0.1 fusion.73
  9.0 0.1 fusion.84
  9.1 0.1 fusion.95
  9.2 2.8 %fusion.10 = (bf16[256,2048]{1,0:T(8,128)(2,1)S(1)}, bf16[256,2048]{1,0:T(8,128)(2,1)S(1)}) fusion(s32[256]{0:T(256)S(1)} %iota.25, s32[2048]{0:T(1024)S(1)} %iota.24), kind=kLoop, calls=%fused_computation.43 | loop fusion | flops 20447232 | bytes 2106368 | tf_op jit(solution)/shard_map/convert_element_type | solution.py:55
  12.0 0.1 constant_dynamic-update-slice_fusion.1
  12.1 0.1 fusion.27
  12.2 0.1 fusion.29
  12.3 0.1 fusion.31
  12.4 0.1 fusion.33
  12.5 0.1 fusion.35
  12.6 0.1 fusion.25
  12.6 0.1 fusion.52
  12.7 0.0 copy-start.5
  12.8 0.1 constant_dynamic-update-slice_fusion
  12.9 0.1 fusion.39
  13.0 0.1 fusion.41
  13.1 6.3 %fusion.2 = (bf16[512,2048]{1,0:T(8,128)(2,1)}, bf16[512,2048]{1,0:T(8,128)(2,1)}) fusion(s32[2048]{0:T(1024)S(1)} %broadcast_add_fusion, s32[512]{0:T(512)S(1)} %broadcast_add_fusion.1), kind=kLoop, calls=%fused_computation.4 | loop fusion | flops 37748736 | bytes 4204544 | tf_op jit(solution)/shard_map/convert_element_type | solution.py:40
  19.4 0.1 fusion.43
  19.5 0.0 copy-done.5
  19.5 0.1 fusion.45
  19.6 0.1 fusion.47
  19.7 0.0 copy-start
  19.7 0.1 fusion.37
  19.7 0.1 fusion.53
  19.9 3.3 %copy-done.6 = bf16[2048,2048]{1,0:T(8,128)(2,1)} copy-done((bf16[2048,2048]{1,0:T(8,128)(2,1)}, bf16[2048,2048]{1,0:T(8,128)(2,1)S(1)}, u32[]{:S(2)}) %copy-start.6) | copy-done | bytes 8388632
  23.1 1.3 %fusion.64 = (bf16[512,512]{1,0:T(8,128)(2,1)}, bf16[512,512]{1,0:T(8,128)(2,1)}) fusion(f32[2,512,512]{2,1,0:T(8,128)S(1)} %copy-done), kind=kLoop, calls=%fused_computation.136 | loop fusion | flops 1048576 | bytes 3145728 | tf_op jit(solution)/shard_map/convert_element_type | solution.py:151
  24.4 9.9 %all-to-all-done = bf16[4,2,128,512]{3,2,1,0:T(8,128)(2,1)S(1)} async-done(((bf16[4,2,128,512]{3,2,1,0:T(8,128)(2,1)}), bf16[4,2,128,512]{3,2,1,0:T(8,128)(2,1)S(1)}, u32[]{:S(2)}, u32[]{:S(2)}) %all-to-all-start) | async-done | bytes 1048608 | tf_op jit(solution)/shard_map/all_to_all | solution.py:153
  34.4 0.8 copy.32
  35.2 1.3 %copy.45 = bf16[32,8,4,512]{3,1,2,0:T(8,128)(2,1)} copy(bf16[32,8,4,512]{3,2,1,0:T(4,128)(2,1)S(1)} %bitcast.81) | data formatting | bytes 2097152
  36.5 3.5 %all-to-all-start.1 = ((bf16[4,128,512]{2,1,0:T(8,128)(2,1)}), bf16[4,128,512]{2,1,0:T(8,128)(2,1)S(1)}, u32[]{:S(2)}, u32[]{:S(2)}) async-start(bf16[4,128,512]{2,1,0:T(8,128)(2,1)} %bitcast.15), calls=%async_computation.1 | async-start | bytes 1048576 | tf_op jit(solution)/shard_map/all_to_all | solution.py:162
  40.0 0.0 copy-start.4
  40.0 6.1 %fusion.107 = f32[256,2048]{1,0:T(8,128)S(1)} fusion(bf16[256,2048]{1,0:T(8,128)(2,1)} %bitcast.85, bf16[2048,2048]{1,0:T(8,128)(2,1)} %copy-done.5), kind=kOutput, calls=%fused_computation.214 | convolution fusion | flops 2147483648 | bytes 11534336 | tf_op jit(solution)/shard_map/dot_general | solution.py:68
  46.1 0.0 copy-done.4
  46.1 7.1 %fusion.106 = f32[256,2048]{1,0:T(8,128)} fusion(bf16[256,2048]{1,0:T(8,128)(2,1)S(1)} %bitcast.86, bf16[2048,2048]{1,0:T(8,128)(2,1)} %copy-done.6), kind=kOutput, calls=%fused_computation.213 | convolution fusion | flops 2147483648 | bytes 11534336 | tf_op jit(solution)/shard_map/dot_general | solution.py:68
  53.2 0.8 all-to-all-done.1
  54.0 4.3 %all-to-all-start.2 = ((bf16[4,128,512]{2,1,0:T(8,128)(2,1)}), bf16[4,128,512]{2,1,0:T(8,128)(2,1)S(1)}, u32[]{:S(2)}, u32[]{:S(2)}) async-start(bf16[4,128,512]{2,1,0:T(8,128)(2,1)} %bitcast.83), calls=%async_computation.2 | async-start | bytes 1048576 | tf_op jit(solution)/shard_map/all_to_all | solution.py:162
  58.3 2.9 %fusion.15 = (bf16[128,2048]{1,0:T(8,128)(2,1)S(1)}, bf16[128,2048]{1,0:T(8,128)(2,1)S(1)}, bf16[128,2048]{1,0:T(8,128)(2,1)S(1)}) fusion(bf16[128,2048]{1,0:T(8,128)(2,1)S(1)} %bitcast.78, f32[256,2048]{1,0:T(8,128)} %fusion.106, f32[256,2048]{1,0:T(8,128)S(1)} %fusion.107), kind=kLoop, calls=%fused_computation.67 | loop fusion | flops 10485760 | bytes 6291456 | tf_op jit(solution)/shard_map/convert_element_type | solution.py:175
  61.2 0.0 slice-start
  61.2 1.3 %fusion.17 = bf16[128,2048]{1,0:T(8,128)(2,1)S(1)} fusion(bf16[128,2048]{1,0:T(8,128)(2,1)S(1)} %get-tuple-element.22, bf16[128,2048]{1,0:T(8,128)(2,1)S(1)} %get-tuple-element.21, bf16[128,2048]{1,0:T(8,128)(2,1)S(1)} %bitcast.79), kind=kLoop, calls=%fused_computation.69 | loop fusion | flops 9437184 | bytes 2097152 | tf_op jit(solution)/shard_map/convert_element_type | solution.py:176
  62.5 0.0 slice-start.1
  62.5 5.9 %fusion.62 = f32[256,2048]{1,0:T(8,128)S(1)} fusion(bf16[2048,2048]{1,0:T(8,128)(2,1)} %copy-done.5, bf16[128,2048]{1,0:T(8,128)(2,1)S(1)} %fusion.17, bf16[128,2048]{1,0:T(8,128)(2,1)S(1)} %get-tuple-element.20), kind=kOutput, calls=%fused_computation.134 | convolution fusion | flops 2149580800 | bytes 11534336 | tf_op jit(solution)/shard_map/dot_general | solution.py:68
  68.5 3.8 %fusion.63 = f32[256,2048]{1,0:T(8,128)} fusion(bf16[2048,2048]{1,0:T(8,128)(2,1)S(1)} %bitcast.92, bf16[128,2048]{1,0:T(8,128)(2,1)S(1)} %fusion.17, bf16[128,2048]{1,0:T(8,128)(2,1)S(1)} %get-tuple-element.20), kind=kOutput, calls=%fused_computation.135 | convolution fusion | flops 2149580800 | bytes 11534336 | tf_op jit(solution)/shard_map/dot_general | solution.py:68
  72.2 0.0 all-to-all-done.2
  72.2 0.2 multiply_bitcast_fusion
  72.4 0.1 copy.44
  72.5 1.3 %copy-done.1 = f32[256,2048]{1,0:T(8,128)S(1)} copy-done((f32[256,2048]{1,0:T(8,128)S(1)}, f32[256,2048]{1,0:T(8,128)}, u32[]{:S(2)}) %copy-start.1) | copy-done | bytes 2097176
  73.8 1.2 %fusion.19 = (bf16[128,2048]{1,0:T(8,128)(2,1)S(1)}, bf16[128,2048]{1,0:T(8,128)(2,1)S(1)}, bf16[128,2048]{1,0:T(8,128)(2,1)S(1)}) fusion(f32[128,2048]{1,0:T(8,128)S(1)} %bitcast.76, f32[256,2048]{1,0:T(8,128)S(1)} %copy-done.1, f32[256,2048]{1,0:T(8,128)S(1)} %fusion.62), kind=kLoop, calls=%fused_computation.71 | loop fusion | flops 9961472 | bytes 6815744 | tf_op jit(solution)/shard_map/convert_element_type | solution.py:175
  75.0 0.0 copy-start.3
  75.0 1.1 %fusion.21 = bf16[128,2048]{1,0:T(8,128)(2,1)S(1)} fusion(bf16[128,2048]{1,0:T(8,128)(2,1)S(1)} %get-tuple-element.19, bf16[128,2048]{1,0:T(8,128)(2,1)S(1)} %get-tuple-element.18, f32[128,2048]{1,0:T(8,128)S(1)} %bitcast.77), kind=kLoop, calls=%fused_computation.73 | loop fusion | flops 8912896 | bytes 2621440 | tf_op jit(solution)/shard_map/convert_element_type | solution.py:176
  76.2 0.4 copy-done.3
  76.6 0.7 fusion.61
  77.4 0.8 copy-done.2
  78.2 0.7 fusion.60
  78.9 0.1 fusion.69
  79.0 0.7 pad_maximum_fusion.9
  79.7 15.0 %column_exchange.1 = bf16[32,32,128]{2,1,0:T(8,128)(2,1)} custom-call(bf16[32,32,128]{2,1,0:T(8,128)(2,1)} %bitcast.87), custom_call_target="tpu_custom_call" | custom-call | tf_op jit(solution)/shard_map/column_exchange/pallas_call | solution.py:127
  94.7 1.3 %convolution_bitcast_fusion = f32[2,16,64,128]{3,2,1,0:T(8,128)S(1)} fusion(bf16[32,2,16,128]{3,2,1,0:T(8,128)(2,1)} %bitcast.88, bf16[1,2,32,64]{3,2,0,1:T(8,128)(2,1)S(1)} %get-tuple-element.36, bf16[1,2,32,64]{3,2,0,1:T(8,128)(2,1)S(1)} %get-tuple-element.35), kind=kOutput, calls=%fused_computation.56 | convolution fusion | flops 33587200 | bytes 1327104 | tf_op jit(solution)/shard_map/skam,kcsf->cafm/dot_general | solution.py:198
  96.0 0.2 add_convert_fusion
  96.2 0.4 convolution_bitcast_fusion.1
  96.6 0.9 reshape.571
  (19 shorter events, 0.1 us)
Async XLA Ops:
  2.3 32.1 %all-to-all-start = ((bf16[4,2,128,512]{3,2,1,0:T(8,128)(2,1)}), bf16[4,2,128,512]{3,2,1,0:T(8,128)(2,1)S(1)}, u32[]{:S(2)}, u32[]{:S(2)}) async-start(bf16[4,2,128,512]{3,2,1,0:T(8,128)(2,1)} %copy.31), calls=%async_computation | async-start | bytes 2097152 | tf_op jit(solution)/shard_map/all_to_all | solution.py:153
  12.7 6.8 %copy-start.5 = (bf16[2048,2048]{1,0:T(8,128)(2,1)}, bf16[2048,2048]{1,0:T(8,128)(2,1)S(1)}, u32[]{:S(2)}) copy-start(bf16[2048,2048]{1,0:T(8,128)(2,1)S(1)} %fusion.52) | copy-start | bytes 25165828
  19.7 3.5 %copy-start = (f32[2,512,512]{2,1,0:T(8,128)S(1)}, f32[2,512,512]{2,1,0:T(8,128)}, u32[]{:S(2)}) copy-start(f32[2,512,512]{2,1,0:T(8,128)} %param.3) | copy-start | bytes 6291460
  19.9 3.3 %copy-start.6 = (bf16[2048,2048]{1,0:T(8,128)(2,1)}, bf16[2048,2048]{1,0:T(8,128)(2,1)S(1)}, u32[]{:S(2)}) copy-start(bf16[2048,2048]{1,0:T(8,128)(2,1)S(1)} %fusion.53) | copy-start | bytes 25165828
  36.5 17.5 %all-to-all-start.1 = ((bf16[4,128,512]{2,1,0:T(8,128)(2,1)}), bf16[4,128,512]{2,1,0:T(8,128)(2,1)S(1)}, u32[]{:S(2)}, u32[]{:S(2)}) async-start(bf16[4,128,512]{2,1,0:T(8,128)(2,1)} %bitcast.15), calls=%async_computation.1 | async-start | bytes 1048576 | tf_op jit(solution)/shard_map/all_to_all | solution.py:162
  40.0 6.1 %copy-start.4 = (bf16[32,8,4,512]{3,1,2,0:T(8,128)(2,1)S(1)}, bf16[32,8,4,512]{3,1,2,0:T(8,128)(2,1)}, u32[]{:S(2)}) copy-start(bf16[32,8,4,512]{3,1,2,0:T(8,128)(2,1)} %copy.45) | copy-start | bytes 3145732
  54.0 18.2 %all-to-all-start.2 = ((bf16[4,128,512]{2,1,0:T(8,128)(2,1)}), bf16[4,128,512]{2,1,0:T(8,128)(2,1)S(1)}, u32[]{:S(2)}, u32[]{:S(2)}) async-start(bf16[4,128,512]{2,1,0:T(8,128)(2,1)} %bitcast.83), calls=%async_computation.2 | async-start | bytes 1048576 | tf_op jit(solution)/shard_map/all_to_all | solution.py:162
  61.2 7.2 %slice-start = ((s8[8388608]{0:T(1024)(128)(4,1)}), s8[4194304]{0:T(1024)(128)(4,1)S(1)}, s32[]{:S(2)}) async-start(s8[8388608]{0:T(1024)(128)(4,1)} %bitcast.91), calls=%async_computation.3 | async-start | bytes 8388608
  62.5 5.9 %slice-start.1 = ((s8[8388608]{0:T(1024)(128)(4,1)}), s8[4194304]{0:T(1024)(128)(4,1)S(1)}, s32[]{:S(2)}) async-start(s8[8388608]{0:T(1024)(128)(4,1)} %bitcast.91), calls=%async_computation.4 | async-start | bytes 8388608
  72.2 1.6 %copy-start.1 = (f32[256,2048]{1,0:T(8,128)S(1)}, f32[256,2048]{1,0:T(8,128)}, u32[]{:S(2)}) copy-start(f32[256,2048]{1,0:T(8,128)} %fusion.63) | copy-start | bytes 6291460
  75.0 1.6 %copy-start.3 = (bf16[512,2048]{1,0:T(8,128)(2,1)S(1)}, bf16[512,2048]{1,0:T(8,128)(2,1)}, u32[]{:S(2)}) copy-start(bf16[512,2048]{1,0:T(8,128)(2,1)} %get-tuple-element.11) | copy-start | bytes 6291460
  76.6 1.6 %copy-start.2 = (bf16[512,2048]{1,0:T(8,128)(2,1)S(1)}, bf16[512,2048]{1,0:T(8,128)(2,1)}, u32[]{:S(2)}) copy-start(bf16[512,2048]{1,0:T(8,128)(2,1)} %get-tuple-element.16) | copy-start | bytes 6291460
